TPU v7x, 512 devices: a whole 4x8x8 slice. The times are simulated.
512 devices in a mesh: section: 16 (over x_lo, z), dp: 32 (over x_hi, y, core).
Axes of the slice: x: 4 (x_hi: 2, x_lo: 2; x = x_hi * 2 + x_lo), y: 8, z: 8, core: 2. Of those that a mesh axis runs over, the one named last changes fastest.
Arguments:
- act_in: float32 [16, 2, 32, 15, 15, 256], P('section', None, 'dp'), may hold values from -6 to 6
- act_mid: float32 [16, 2, 32, 15, 15, 256], P('section', None, 'dp'), may hold values from 0 to 2
- relu_mask: int32 [16, 2, 32, 15, 15, 256], P('section', None, 'dp'), may hold values 0 or 1
- arriving: float32 [16, 32, 15, 15, 256], P('section', 'dp'), may hold values from -6 to 6
- loss_grad: float32 [1, 32, 15, 15, 256], P(None, 'dp'), may hold values from -6 to 6
- w_first: float32 [16, 1792, 256], P('section', 'dp'), may hold values from -0.125 to 0.125
- w_second: float32 [16, 1792, 256], P('section', 'dp'), may hold values from -0.125 to 0.125
Outputs:
- data_grad: float32 [16, 2, 32, 15, 15, 256], P('section', None, 'dp')
- first_grad: float32 [16, 1792, 256], P('section', 'dp')
- second_grad: float32 [16, 1792, 256], P('section', 'dp')
All inputs are finite; a program needn't handle non-finite values. No bound on the sum of `relu_mask` on one device may be relied on, other than what follows from the above.
Results may differ from a plain program's by a relative error of at most 0.00011.
Values sent between devices are 32-bit elements; how exact they have to be, the bound alone decides.
A program may use at most 64 MiB of HBM per device.

v0:
```python
import jax
import jax.numpy as jnp
from jax import lax
from jax.sharding import PartitionSpec as P


def shifted(shard, axis, by):
    peers = lax.axis_size(axis)
    pairs = [(i, i + by) for i in range(peers) if 0 <= i + by < peers]
    return lax.ppermute(shard, axis, pairs)


def spread_taps(values, spatial):
    widths = [(0, 0)] * 4
    widths[spatial] = (3, 3)
    padded = jnp.pad(values, widths)
    extent = values.shape[spatial]
    pieces = [
        lax.slice_in_dim(padded, offset, offset + extent, axis=spatial) for offset in range(7)
    ]
    return jnp.concatenate(pieces, axis=-1)


def fold_taps(products, spatial):
    channels = products.shape[-1] // 7
    widths = [(0, 0)] * 4
    widths[spatial] = (3, 3)
    padded = jnp.pad(products, widths)
    extent = products.shape[spatial]
    summed = jnp.zeros(products.shape[:-1] + (channels,), products.dtype)
    for offset in range(7):
        window = lax.slice_in_dim(padded, 6 - offset, 6 - offset + extent, axis=spatial)
        summed = summed + window[..., offset * channels : (offset + 1) * channels]
    return summed


def project_taps(values, weight):
    return jnp.einsum("nhwc,kc->nhwk", values, weight, precision=lax.Precision.HIGHEST)


def flat_patches(values, spatial):
    patches = spread_taps(values.reshape((-1,) + values.shape[2:]), spatial)
    return patches.reshape(-1, patches.shape[-1])


def correlate(patches, grad_rows, mean_scale):
    return jnp.einsum("rk,rc->kc", patches, grad_rows, precision=lax.Precision.HIGHEST) * mean_scale


def local(act_in, act_mid, relu_mask, arriving, loss_grad, w_first, w_second):
    tick_count = act_in.shape[1]
    channels = act_in.shape[-1]
    is_last = lax.axis_index("section") == lax.axis_size("section") - 1
    full_first, full_second = (
        lax.all_gather(w_first[0], "dp", axis=0, tiled=True),
        lax.all_gather(w_second[0], "dp", axis=0, tiled=True),
    )
    incoming = arriving[0]
    mid_grad = fold_taps(project_taps(incoming, full_second), 1)
    in_list = [incoming]
    pre_list = []
    out_list = []
    for tick_index in range(tick_count):
        if tick_index > 0:
            from_above = shifted(out_list[-1], "section", -1)
            incoming = jnp.where(is_last, loss_grad[tick_index - 1], from_above)
            in_list.append(incoming)
            mid_grad = fold_taps(project_taps(incoming, full_second), 1)
        pre_grad = mid_grad * relu_mask[0, tick_index].astype(jnp.float32)
        out_list.append(fold_taps(project_taps(pre_grad, full_first), 2))
        pre_list.append(pre_grad)
    data_grad = jnp.stack(out_list, axis=0)[None]
    mean_scale = 1.0 / (tick_count * act_in.shape[2] * lax.axis_size("dp"))
    first_patches = flat_patches(act_in[0], 2)
    second_patches = flat_patches(act_mid[0], 1)
    pre_rows = jnp.stack(pre_list, axis=0).reshape(-1, channels)
    in_rows = jnp.stack(in_list, axis=0).reshape(-1, channels)
    summed = lax.psum_scatter(
        jnp.concatenate(
            [
                correlate(first_patches, pre_rows, mean_scale),
                correlate(second_patches, in_rows, mean_scale),
            ],
            axis=1,
        ),
        "dp",
        scatter_dimension=0,
        tiled=True,
    )
    first_grad = summed[:, :channels]
    second_grad = summed[:, channels:]
    return (data_grad, first_grad[None], second_grad[None])


def solution(mesh):
    return jax.shard_map(
        local,
        mesh=mesh,
        in_specs=(
            P("section", None, "dp", None, None, None),
            P("section", None, "dp", None, None, None),
            P("section", None, "dp", None, None, None),
            P("section", "dp", None, None, None),
            P(None, "dp", None, None, None),
            P("section", "dp", None),
            P("section", "dp", None),
        ),
        out_specs=(
            P("section", None, "dp", None, None, None),
            P("section", "dp", None),
            P("section", "dp", None),
        ),
        check_vma=False,
    )
```

profile of v0, /device:TPU:16, one launch (start us, length us, event | category | flops | bytes accessed | tf_op | source)
XLA Modules:
  0.0 363.2 jit_solution(2133980787343362848)
XLA Ops:
  8.7 1.3 copy.89
  10.0 2.1 reduce.1
  12.1 2.0 copy.90
  14.1 2.1 reduce
  16.3 1.7 pad_slice_fusion.24
  22.4 1.6 copy.54
  24.0 4.0 %pad_slice_fusion.30 = (f32[2,15,15,256]{3,0,2,1:T(2,128)}, f32[2,15,15,256]{3,0,2,1:T(2,128)}, f32[2,15,15,256]{3,0,2,1:T(2,128)}, f32[2,15,15,256]{3,0,2,1:T(2...) fusion(f32[2,15,15,256]{3,0,2,1:T(2,128)} %bitcast.66), kind=kLoop, calls=%fused_computation.46 | loop fusion | bytes 3225600 | tf_op jit(solution)/shard_map/slice | solution.py:19
  39.2 1.9 constant_dynamic-update-slice_fusion.6
  50.6 48.9 %all-gather.5.cloned.1.call-done = f32[1,1792,256]{2,1,0:T(8,128)} async-done(((f32[1,56,256]{2,1,0:T(8,128)}), f32[1,1792,256]{2,1,0:T(8,128)}) %all-gather.5.cloned.1.call-update) | async-done | bytes 1835024 | tf_op jit(solution)/shard_map/all_gather | solution.py:56
  99.5 3.2 convolution_bitcast_fusion.3
  102.8 81.2 %all-gather.7.cloned.1.call-done = f32[1,1792,256]{2,1,0:T(8,128)} async-done(((f32[1,56,256]{2,1,0:T(8,128)}), f32[1,1792,256]{2,1,0:T(8,128)}) %all-gather.7.cloned.1.call-update) | async-done | bytes 1835024 | tf_op jit(solution)/shard_map/all_gather | solution.py:55
  184.1 3.3 convolution_bitcast_fusion.2
  187.6 1.6 collective-permute-start
  190.9 6.8 %collective-permute-done = f32[1,15,15,256]{3,2,1,0:T(8,128)S(1)} collective-permute-done((f32[1,15,15,256]{3,2,1,0:T(8,128)S(1)}, f32[1,15,15,256]{3,2,1,0:T(8,128)S(1)}, u32[]{:S(2)}, u32[]{:S(2)}) %collective-permute-start) | collective-permute-done | bytes 230432 | tf_op jit(solution)/shard_map/ppermute | solution.py:10
  199.2 1.9 reshape.78
  201.1 2.8 convolution_bitcast_fusion.1
  204.9 5.2 %convolution_multiply_fusion = f32[1792,256]{0,1:T(8,128)S(1)} fusion(f32[450,1792]{1,0:T(8,128)} %constant_dynamic-update-slice_fusion.7, f32[450,256]{1,0:T(8,128)S(1)} %copy-done.13), kind=kOutput, calls=%fused_computation.25 | convolution fusion | flops 2477719552 | bytes 5521408 | tf_op jit(solution)/shard_map/rk,rc->kc/dot_general | solution.py:47
  210.0 5.3 %convolution_multiply_fusion.1 = f32[1792,256]{0,1:T(8,128)S(1)} fusion(f32[450,1792]{1,0:T(8,128)} %constant_dynamic-update-slice_fusion, f32[450,256]{1,0:T(8,128)S(1)} %reshape.77), kind=kOutput, calls=%fused_computation.26 | convolution fusion | flops 2477719552 | bytes 5521408 | tf_op jit(solution)/shard_map/rk,rc->kc/dot_general | solution.py:47
  215.3 2.1 pad_maximum_fusion
  217.4 5.2 %copy.58 = f32[1792,512]{1,0:T(8,128)} copy(f32[1792,512]{0,1:T(8,128)} %pad_maximum_fusion) | data formatting | bytes 7340032
  222.8 1.3 copy-done
  224.1 2.6 convolution_bitcast_fusion
  226.9 1.2 copy.55
  228.2 126.0 %reduce-scatter.4.cloned.1.call-done = f32[56,512]{1,0:T(8,128)} async-done(((f32[1792,512]{1,0:T(8,128)}), f32[56,512]{1,0:T(8,128)}) %reduce-scatter.4.cloned.1.call-update) | async-done | bytes 114704
  (102 shorter events, 33.7 us)
Async XLA Ops:
  7.2 92.3 %all-gather.5.cloned.1.call-start = ((), (), s32[]{:S(2)}) async-start(), calls=%async_computation.1 | async-start | bytes 1892352 | tf_op jit(solution)/shard_map/all_gather | solution.py:56
  7.9 176.2 %all-gather.7.cloned.1.call-start = ((), (), s32[]{:S(2)}) async-start(), calls=%async_computation.2 | async-start | bytes 1892352 | tf_op jit(solution)/shard_map/all_gather | solution.py:55
  8.6 345.5 %reduce-scatter.4.cloned.1.call-start = ((), (), s32[]{:S(2)}) async-start(), calls=%async_computation.3 | async-start | bytes 3784704
  32.8 4.7 %copy-start.14 = (f32[2,15,15,256]{3,0,2,1:T(2,128)S(1)}, f32[2,15,15,256]{3,0,2,1:T(2,128)}, u32[]{:S(2)}) copy-start(f32[2,15,15,256]{3,0,2,1:T(2,128)} %get-tuple-element.12) | copy-start | bytes 1382404
  37.5 7.0 %copy-start.6 = (f32[450,256]{1,0:T(8,128)S(1)}, f32[450,256]{1,0:T(8,128)}, u32[]{:S(2)}) copy-start(f32[450,256]{1,0:T(8,128)} %concatenate.52) | copy-start | bytes 1382404
  38.4 7.0 %copy-start.8 = (f32[450,256]{1,0:T(8,128)S(1)}, f32[450,256]{1,0:T(8,128)}, u32[]{:S(2)}) copy-start(f32[450,256]{1,0:T(8,128)} %concatenate.53) | copy-start | bytes 1382404
  39.2 7.0 %copy-start.9 = (f32[450,256]{1,0:T(8,128)S(1)}, f32[450,256]{1,0:T(8,128)}, u32[]{:S(2)}) copy-start(f32[450,256]{1,0:T(8,128)} %concatenate.40) | copy-start | bytes 1382404
  41.2 5.9 %copy-start.11 = (f32[450,256]{1,0:T(8,128)S(1)}, f32[450,256]{1,0:T(8,128)}, u32[]{:S(2)}) copy-start(f32[450,256]{1,0:T(8,128)} %concatenate.41) | copy-start | bytes 1382404
  42.0 5.9 %copy-start.10 = (f32[450,256]{1,0:T(8,128)S(1)}, f32[450,256]{1,0:T(8,128)}, u32[]{:S(2)}) copy-start(f32[450,256]{1,0:T(8,128)} %concatenate.42) | copy-start | bytes 1382404
  42.9 5.9 %copy-start.12 = (f32[450,256]{1,0:T(8,128)S(1)}, f32[450,256]{1,0:T(8,128)}, u32[]{:S(2)}) copy-start(f32[450,256]{1,0:T(8,128)} %concatenate.43) | copy-start | bytes 1382404
  43.7 5.9 %copy-start.20 = (s32[1,2,1,15,15,256]{5,2,4,3,1,0:T(1,128)S(1)}, s32[1,2,1,15,15,256]{5,2,4,3,1,0:T(1,128)}, u32[]{:S(2)}) copy-start(s32[1,2,1,15,15,256]{5,2,4,3,1,0:T(1,128)} %param.9) | copy-start | bytes 1382404
  44.6 54.9 %copy-start.16 = (f32[1,1,15,15,256]{4,1,3,2,0:T(1,128)S(1)}, f32[1,1,15,15,256]{4,1,3,2,0:T(1,128)}, u32[]{:S(2)}) copy-start(f32[1,1,15,15,256]{4,1,3,2,0:T(1,128)} %param.10) | copy-start | bytes 691204
  102.8 81.3 %copy-start.2 = (f32[1,15,15,256]{3,2,1,0:T(8,128)}, f32[1,15,15,256]{3,2,1,0:T(8,128)S(1)}, u32[]{:S(2)}) copy-start(f32[1,15,15,256]{3,2,1,0:T(8,128)S(1)} %fusion.10) | copy-start | bytes 691204
  184.1 5.1 %copy-start.5 = (f32[450,256]{1,0:T(8,128)S(1)}, f32[450,256]{1,0:T(8,128)}, u32[]{:S(2)}) copy-start(f32[450,256]{1,0:T(8,128)} %concatenate.44) | copy-start | bytes 1382404
  184.1 5.9 %copy-start.7 = (f32[450,256]{1,0:T(8,128)S(1)}, f32[450,256]{1,0:T(8,128)}, u32[]{:S(2)}) copy-start(f32[450,256]{1,0:T(8,128)} %concatenate.45) | copy-start | bytes 1382404
  184.1 13.6 %copy-start.15 = (f32[1,1,15,15,256]{4,1,3,2,0:T(1,128)S(1)}, f32[1,1,15,15,256]{4,1,3,2,0:T(1,128)}, u32[]{:S(2)}) copy-start(f32[1,1,15,15,256]{4,1,3,2,0:T(1,128)} %param.11) | copy-start | bytes 691204
  187.4 11.0 %copy-start.18 = (f32[1,1,15,15,256]{4,3,2,1,0:T(8,128)S(1)}, f32[1,1,15,15,256]{4,3,2,1,0:T(8,128)}, u32[]{:S(2)}) copy-start(f32[1,1,15,15,256]{4,3,2,1,0:T(8,128)} %copy.54) | copy-start | bytes 691204
  187.4 13.7 %copy-start.1 = (f32[1,1792,256]{2,1,0:T(8,128)S(1)}, f32[1,1792,256]{2,1,0:T(8,128)}, u32[]{:S(2)}) copy-start(f32[1,1792,256]{2,1,0:T(8,128)} %all-gather.5.cloned.1.call-done) | copy-start | bytes 5505028
  187.6 10.1 %collective-permute-start = (f32[1,15,15,256]{3,2,1,0:T(8,128)S(1)}, f32[1,15,15,256]{3,2,1,0:T(8,128)S(1)}, u32[]{:S(2)}, u32[]{:S(2)}) collective-permute-start(f32[1,15,15,256]{3,2,1,0:T(8,128)S(1)} %fusion.23), channel_id=1, source_target_pairs={{32,0},{64,32},{96,64},{128,96},{160,128},{192,160},{224,192},{256... | collective-permute-start | bytes 691208 | tf_op jit(solution)/shard_map/ppermute | solution.py:10
  201.1 2.8 copy-start.19
  201.1 3.6 %copy-start.3 = (f32[1,15,15,256]{3,2,1,0:T(8,128)S(1)}, f32[1,15,15,256]{3,2,1,0:T(8,128)}, u32[]{:S(2)}) copy-start(f32[1,15,15,256]{3,2,1,0:T(8,128)} %copy-done.2) | copy-start | bytes 691204
  203.9 1.0 copy-start.13
  204.0 0.7 copy-start.4
  222.6 1.5 copy-start
  (1 other events, 0.7 us)
Sparse Core Ops, SparseCore 0:
  11.3 88.1 all-gather.4
  102.8 81.1 all-gather.6
  222.7 131.3 reduce-scatter.3
where the time goes:
time: 364 us; the launch traced here: 363 us
  waiting for transfers between devices  264 us (73%)
  local copies, waits for them, and re-layouts  52.7 us (14%)
  matrix products  22.3 us (6%)
  between operations  14.1 us (4%)
  other arithmetic  8.07 us (2%)
    unnamed x4, waiting for transfers between devices  127 us
    all_gather x1, waiting for transfers between devices, local(): lax.all_gather(w_first[0], 'dp', axis=0, tiled=True)  81.2 us
    all_gather x1, waiting for transfers between devices, local(): lax.all_gather(w_second[0], 'dp', axis=0, tiled=True)  48.9 us
    unnamed x63, local copies, waits for them, and re-layouts  26.9 us
    slice x14, local copies, waits for them, and re-layouts, spread_taps(): lax.slice_in_dim(padded, offset, offset + extent, axis=spatial)  12.5 us
    dot_general x4, matrix products, project_taps(): jnp.einsum('nhwc,kc->nhwk', values, weight, precision=lax.Precision.HIGHEST)  11.9 us
    dot_general x2, matrix products, correlate(): jnp.einsum('rk,rc->kc', patches, grad_rows, precision=lax.Precision.HIGHEST)  10.4 us
    concatenate x16, local copies, waits for them, and re-layouts, spread_taps(): return jnp.concatenate(pieces, axis=-1)  9.53 us
  transfers between devices with their start and end apart: 4, of which 4 were waited for; matrix products, arithmetic and copies ran while one was open for 14% of the time, Pallas kernels for 0%

commit v1 on v0

--- a/solution.py
+++ b/solution.py
@@ -53,7 +53,9 @@
     is_last = lax.axis_index("section") == lax.axis_size("section") - 1
     full_first, full_second = (
         lax.all_gather(w_first[0], "dp", axis=0, tiled=True),
-        lax.all_gather(w_second[0], "dp", axis=0, tiled=True),
+        jnp.concatenate(
+            lax.all_to_all(jnp.stack([w_second[0]] * lax.axis_size("dp")), "dp", 0, 0), axis=0
+        ),
     )
     incoming = arriving[0]
     mid_grad = fold_taps(project_taps(incoming, full_second), 1)

time: 364 us -> 295 us (0.81)
  waiting for transfers between devices: 264 us -> 180 us
  starting transfers between devices: 1.72 us -> 11.6 us
  local copies, waits for them, and re-layouts: 52.7 us -> 59.1 us
    all_gather x1 -> x0, waiting for transfers between devices: 48.9 us -> none  [local(): lax.all_gather(w_second[0], 'dp', axis=0, tiled=True)]
    all_gather x1, waiting for transfers between devices: 81.2 us -> 46.7 us  [local(): lax.all_gather(w_first[0], 'dp', axis=0, tiled=True)]
    all_to_all x0 -> x1, starting transfers between devices: none -> 10.1 us  [local(): lax.all_to_all(jnp.stack([w_second[0]] * lax.axis_size('dp')), 'dp', 0, 0)]
    concatenate x16, local copies, waits for them, and re-layouts: 9.53 us -> 13.5 us  [spread_taps(): return jnp.concatenate(pieces, axis=-1)]
    unnamed x63 -> x71, local copies, waits for them, and re-layouts: 26.9 us -> 26 us
    unnamed x4 -> x3, waiting for transfers between devices: 127 us -> 127 us
  transfers between devices with their start and end apart: 4 -> 4, of which waited for: 4 -> 3; matrix products, arithmetic and copies ran while one was open for 14% -> 18% of each run, Pallas kernels for 0% -> 0%
where the time goes in v1:
time: 295 us; the launch traced here: 294 us
  waiting for transfers between devices  180 us (61%)
  local copies, waits for them, and re-layouts  59.1 us (20%)
  matrix products  20.9 us (7%)
  between operations  14.4 us (5%)
  starting transfers between devices  11.6 us (4%)
  other arithmetic  7.72 us (3%)
    unnamed x3, waiting for transfers between devices  127 us
    all_gather x1, waiting for transfers between devices, local(): lax.all_gather(w_first[0], 'dp', axis=0, tiled=True)  46.7 us
    unnamed x71, local copies, waits for them, and re-layouts  26 us
    slice x14, local copies, waits for them, and re-layouts, spread_taps(): lax.slice_in_dim(padded, offset, offset + extent, axis=spatial)  13.6 us
    concatenate x16, local copies, waits for them, and re-layouts, spread_taps(): return jnp.concatenate(pieces, axis=-1)  13.5 us
    dot_general x4, matrix products, project_taps(): jnp.einsum('nhwc,kc->nhwk', values, weight, precision=lax.Precision.HIGHEST)  10.5 us
    dot_general x2, matrix products, correlate(): jnp.einsum('rk,rc->kc', patches, grad_rows, precision=lax.Precision.HIGHEST)  10.4 us
    all_to_all x1, starting transfers between devices, local(): lax.all_to_all(jnp.stack([w_second[0]] * lax.axis_size('dp')), 'dp', 0, 0)  10.1 us
  transfers between devices with their start and end apart: 4, of which 3 were waited for; matrix products, arithmetic and copies ran while one was open for 18% of the time, Pallas kernels for 0%

profile of v1, /device:TPU:16, one launch (start us, length us, event | category | flops | bytes accessed | tf_op | source)
XLA Modules:
  0.0 294.0 jit_solution(2443735970570894730)
XLA Ops:
  7.2 2.2 stack.27
  9.4 10.1 %all-to-all-start = ((f32[32,56,256]{2,1,0:T(8,128)}), f32[32,56,256]{2,1,0:T(8,128)S(1)}, u32[]{:S(2)}, u32[]{:S(2)}) async-start(f32[32,56,256]{2,1,0:T(8,128)} %stack.27), calls=%async_computation | async-start | bytes 3670016 | tf_op jit(solution)/shard_map/all_to_all | solution.py:57
  21.6 2.1 copy.90
  23.6 2.1 reduce
  25.8 1.8 pad_slice_fusion.24
  33.2 1.1 copy.51
  39.7 1.8 pad_slice_fusion.30
  52.8 1.9 constant_dynamic-update-slice_fusion.6
  55.5 1.9 constant_dynamic-update-slice_fusion.11
  65.3 1.7 convolution_bitcast_fusion.3
  67.8 46.7 %all-gather.3.cloned.1.call-done = f32[1,1792,256]{2,1,0:T(8,128)} async-done(((f32[1,56,256]{2,1,0:T(8,128)}), f32[1,1792,256]{2,1,0:T(8,128)}) %all-gather.3.cloned.1.call-update) | async-done | bytes 1835024 | tf_op jit(solution)/shard_map/all_gather | solution.py:55
  114.5 3.4 %convolution_bitcast_fusion.2 = f32[1,15,15,1792]{3,2,1,0:T(8,128)S(1)} fusion(f32[1,1792,256]{2,1,0:T(8,128)} %all-gather.3.cloned.1.call-done, f32[1,15,15,256]{3,2,1,0:T(8,128)} %fusion.8), kind=kOutput, calls=%fused_computation.29 | convolution fusion | flops 1238630400 | bytes 3678208 | tf_op jit(solution)/shard_map/nhwc,kc->nhwk/dot_general | solution.py:38
  118.1 1.5 collective-permute-start
  121.3 6.8 %collective-permute-done = f32[1,15,15,256]{3,2,1,0:T(8,128)S(1)} collective-permute-done((f32[1,15,15,256]{3,2,1,0:T(8,128)S(1)}, f32[1,15,15,256]{3,2,1,0:T(8,128)S(1)}, u32[]{:S(2)}, u32[]{:S(2)}) %collective-permute-start) | collective-permute-done | bytes 230432 | tf_op jit(solution)/shard_map/ppermute | solution.py:10
  129.6 1.9 reshape.83
  131.4 2.8 convolution_bitcast_fusion.1
  135.2 5.2 %convolution_multiply_fusion = f32[1792,256]{0,1:T(8,128)S(1)} fusion(f32[450,1792]{1,0:T(8,128)} %constant_dynamic-update-slice_fusion.7, f32[450,256]{1,0:T(8,128)S(1)} %copy-done.15), kind=kOutput, calls=%fused_computation.25 | convolution fusion | flops 2477719552 | bytes 5521408 | tf_op jit(solution)/shard_map/rk,rc->kc/dot_general | solution.py:47
  140.4 5.3 %convolution_multiply_fusion.1 = f32[1792,256]{0,1:T(8,128)S(1)} fusion(f32[450,1792]{1,0:T(8,128)} %constant_dynamic-update-slice_fusion, f32[450,256]{1,0:T(8,128)S(1)} %reshape.82), kind=kOutput, calls=%fused_computation.26 | convolution fusion | flops 2477719552 | bytes 5521408 | tf_op jit(solution)/shard_map/rk,rc->kc/dot_general | solution.py:47
  145.7 2.1 pad_maximum_fusion
  147.8 5.2 %copy.58 = f32[1792,512]{1,0:T(8,128)} copy(f32[1792,512]{0,1:T(8,128)} %pad_maximum_fusion) | data formatting | bytes 7340032
  153.2 1.3 copy-done
  154.4 2.6 convolution_bitcast_fusion
  157.3 1.2 copy.55
  158.6 126.1 %reduce-scatter.4.cloned.1.call-done = f32[56,512]{1,0:T(8,128)} async-done(((f32[1792,512]{1,0:T(8,128)}), f32[56,512]{1,0:T(8,128)}) %reduce-scatter.4.cloned.1.call-update) | async-done | bytes 114704
  (110 shorter events, 40.9 us)
Async XLA Ops:
  7.2 13.1 %copy-start.17 = (f32[1,2,1,15,15,256]{5,2,4,3,1,0:T(1,128)S(1)}, f32[1,2,1,15,15,256]{5,2,4,3,1,0:T(1,128)}, u32[]{:S(2)}) copy-start(f32[1,2,1,15,15,256]{5,2,4,3,1,0:T(1,128)} %param.8) | copy-start | bytes 1382404
  9.4 55.9 %all-to-all-start = ((f32[32,56,256]{2,1,0:T(8,128)}), f32[32,56,256]{2,1,0:T(8,128)S(1)}, u32[]{:S(2)}, u32[]{:S(2)}) async-start(f32[32,56,256]{2,1,0:T(8,128)} %stack.27), calls=%async_computation | async-start | bytes 3670016 | tf_op jit(solution)/shard_map/all_to_all | solution.py:57
  19.4 95.0 %all-gather.3.cloned.1.call-start = ((), (), s32[]{:S(2)}) async-start(), calls=%async_computation.2 | async-start | bytes 1892352 | tf_op jit(solution)/shard_map/all_gather | solution.py:55
  20.2 264.5 %reduce-scatter.4.cloned.1.call-start = ((), (), s32[]{:S(2)}) async-start(), calls=%async_computation.3 | async-start | bytes 3784704
  32.4 6.6 %copy-start.20 = (f32[1,1,15,15,256]{4,1,3,2,0:T(1,128)S(1)}, f32[1,1,15,15,256]{4,1,3,2,0:T(1,128)}, u32[]{:S(2)}) copy-start(f32[1,1,15,15,256]{4,1,3,2,0:T(1,128)} %param.10) | copy-start | bytes 691204
  33.2 6.5 %copy-start.16 = (f32[1,2,1,15,15,256]{5,1,4,3,2,0:T(2,128)S(1)}, f32[1,2,1,15,15,256]{5,1,4,3,2,0:T(2,128)}, u32[]{:S(2)}) copy-start(f32[1,2,1,15,15,256]{5,1,4,3,2,0:T(2,128)} %copy.90) | copy-start | bytes 1382404
  41.6 5.6 %copy-start.18 = (f32[2,15,15,256]{3,0,2,1:T(2,128)S(1)}, f32[2,15,15,256]{3,0,2,1:T(2,128)}, u32[]{:S(2)}) copy-start(f32[2,15,15,256]{3,0,2,1:T(2,128)} %get-tuple-element.15) | copy-start | bytes 1382404
  46.3 5.6 %copy-start.4 = (f32[450,256]{1,0:T(8,128)S(1)}, f32[450,256]{1,0:T(8,128)}, u32[]{:S(2)}) copy-start(f32[450,256]{1,0:T(8,128)} %concatenate.47) | copy-start | bytes 1382404
  47.2 7.5 %copy-start.5 = (f32[450,256]{1,0:T(8,128)S(1)}, f32[450,256]{1,0:T(8,128)}, u32[]{:S(2)}) copy-start(f32[450,256]{1,0:T(8,128)} %concatenate.48) | copy-start | bytes 1382404
  52.0 5.5 %copy-start.6 = (f32[450,256]{1,0:T(8,128)S(1)}, f32[450,256]{1,0:T(8,128)}, u32[]{:S(2)}) copy-start(f32[450,256]{1,0:T(8,128)} %concatenate.50) | copy-start | bytes 1382404
  52.0 6.3 %copy-start.7 = (f32[450,256]{1,0:T(8,128)S(1)}, f32[450,256]{1,0:T(8,128)}, u32[]{:S(2)}) copy-start(f32[450,256]{1,0:T(8,128)} %concatenate.51) | copy-start | bytes 1382404
  52.0 7.2 %copy-start.9 = (f32[450,256]{1,0:T(8,128)S(1)}, f32[450,256]{1,0:T(8,128)}, u32[]{:S(2)}) copy-start(f32[450,256]{1,0:T(8,128)} %concatenate.52) | copy-start | bytes 1382404
  52.0 8.0 %copy-start.10 = (f32[450,256]{1,0:T(8,128)S(1)}, f32[450,256]{1,0:T(8,128)}, u32[]{:S(2)}) copy-start(f32[450,256]{1,0:T(8,128)} %concatenate.53) | copy-start | bytes 1382404
  52.8 8.0 %copy-start.11 = (f32[450,256]{1,0:T(8,128)S(1)}, f32[450,256]{1,0:T(8,128)}, u32[]{:S(2)}) copy-start(f32[450,256]{1,0:T(8,128)} %concatenate.40) | copy-start | bytes 1382404
  54.7 7.0 %copy-start.13 = (f32[450,256]{1,0:T(8,128)S(1)}, f32[450,256]{1,0:T(8,128)}, u32[]{:S(2)}) copy-start(f32[450,256]{1,0:T(8,128)} %concatenate.41) | copy-start | bytes 1382404
  55.5 7.0 %copy-start.12 = (f32[450,256]{1,0:T(8,128)S(1)}, f32[450,256]{1,0:T(8,128)}, u32[]{:S(2)}) copy-start(f32[450,256]{1,0:T(8,128)} %concatenate.42) | copy-start | bytes 1382404
  57.4 6.0 %copy-start.14 = (f32[450,256]{1,0:T(8,128)S(1)}, f32[450,256]{1,0:T(8,128)}, u32[]{:S(2)}) copy-start(f32[450,256]{1,0:T(8,128)} %concatenate.43) | copy-start | bytes 1382404
  58.3 6.0 %copy-start.24 = (s32[1,2,1,15,15,256]{5,2,4,3,1,0:T(1,128)S(1)}, s32[1,2,1,15,15,256]{5,2,4,3,1,0:T(1,128)}, u32[]{:S(2)}) copy-start(s32[1,2,1,15,15,256]{5,2,4,3,1,0:T(1,128)} %param.9) | copy-start | bytes 1382404
  114.5 5.1 %copy-start.3 = (f32[450,256]{1,0:T(8,128)S(1)}, f32[450,256]{1,0:T(8,128)}, u32[]{:S(2)}) copy-start(f32[450,256]{1,0:T(8,128)} %concatenate.44) | copy-start | bytes 1382404
  114.5 5.9 %copy-start.8 = (f32[450,256]{1,0:T(8,128)S(1)}, f32[450,256]{1,0:T(8,128)}, u32[]{:S(2)}) copy-start(f32[450,256]{1,0:T(8,128)} %concatenate.45) | copy-start | bytes 1382404
  114.5 13.6 %copy-start.19 = (f32[1,1,15,15,256]{4,1,3,2,0:T(1,128)S(1)}, f32[1,1,15,15,256]{4,1,3,2,0:T(1,128)}, u32[]{:S(2)}) copy-start(f32[1,1,15,15,256]{4,1,3,2,0:T(1,128)} %param.11) | copy-start | bytes 691204
  117.9 10.9 %copy-start.22 = (f32[1,1,15,15,256]{4,3,2,1,0:T(8,128)S(1)}, f32[1,1,15,15,256]{4,3,2,1,0:T(8,128)}, u32[]{:S(2)}) copy-start(f32[1,1,15,15,256]{4,3,2,1,0:T(8,128)} %copy.54) | copy-start | bytes 691204
  118.1 10.0 %collective-permute-start = (f32[1,15,15,256]{3,2,1,0:T(8,128)S(1)}, f32[1,15,15,256]{3,2,1,0:T(8,128)S(1)}, u32[]{:S(2)}, u32[]{:S(2)}) collective-permute-start(f32[1,15,15,256]{3,2,1,0:T(8,128)S(1)} %fusion.21), channel_id=1, source_target_pairs={{32,0},{64,32},{96,64},{128,96},{160,128},{192,160},{224,192},{256... | collective-permute-start | bytes 691208 | tf_op jit(solution)/shard_map/ppermute | solution.py:10
  131.4 3.6 %copy-start.1 = (f32[1,15,15,256]{3,2,1,0:T(8,128)S(1)}, f32[1,15,15,256]{3,2,1,0:T(8,128)}, u32[]{:S(2)}) copy-start(f32[1,15,15,256]{3,2,1,0:T(8,128)} %fusion.8) | copy-start | bytes 691204
  (5 other events, 6.7 us)
Sparse Core Ops, SparseCore 0:
  23.6 90.8 all-gather.2
  153.1 131.5 reduce-scatter.3
